TPU v7x, 32 devices: a whole 2x2x4 slice. The times are simulated.
32 devices in a mesh: grp: 4 (over y, core), ch: 8 (over z, x).
Axes of the slice: x: 2, y: 2, z: 4, core: 2. Of those that a mesh axis runs over, the one named last changes fastest.
Arguments:
- strain: bfloat16 [8, 1024, 4096], P('grp', 'ch'), may hold values from -6 to 6
- valid_mask: int32 [8, 1024], P('grp', 'ch'), may hold values 0 or 1
- pair_list: int32 [8, 6, 2], P('ch'), may hold values from 0 to 7, as said below
- owner_group: int32 [8, 6], P('ch'), may hold values from 0 to 3, as said below
Outputs:
- stacks: float32 [4, 8, 2, 128, 4096], P('grp', 'ch')
Inputs may be any that keep to these rules, and one draw needn't show every extreme that they name: `pair_list`: entries are channel block numbers; each ordered pair of blocks appears at most once over all columns. `owner_group`: in each column no group owns more than 2 entries, and some group owns exactly 2.
All inputs are finite; a program needn't handle non-finite values. No bound on the sum of `valid_mask` on one device may be relied on, other than what follows from the above.
Results may differ from a plain program's by a relative error of at most 0.0042.
Values may be sent and summed in bfloat16 or wider, within the bound.
A program may use at most 192 MiB of HBM per device.

v0:
```python
import math
import jax
import jax.numpy as jnp
from jax import lax
from jax.sharding import PartitionSpec as P

NFFT = 4096
NB = 1024
SUB = 64
BLK = 128
CAP = 2


def forward_table(length, bins):
    samples = jnp.arange(length, dtype=jnp.int32)
    frequency = jnp.arange(1, bins + 1, dtype=jnp.int32)
    angles = jnp.mod(samples[:, None] * frequency[None, :], length).astype(jnp.float32) * (
        2.0 * math.pi / length
    )
    hann_taper = 0.5 - 0.5 * jnp.cos(samples.astype(jnp.float32) * (2.0 * math.pi / length))
    return jnp.concatenate(
        [hann_taper[:, None] * jnp.cos(angles), -hann_taper[:, None] * jnp.sin(angles)], axis=1
    ).astype(jnp.bfloat16)


def inverse_table(length, bins):
    frequency = jnp.arange(1, bins + 1, dtype=jnp.int32)
    lag_index = jnp.arange(length, dtype=jnp.int32) - length // 2
    angles = jnp.mod(frequency[:, None] * lag_index[None, :], length).astype(jnp.float32) * (
        2.0 * math.pi / length
    )
    return jnp.concatenate([jnp.cos(angles), -jnp.sin(angles)], axis=0)


def whiten_rows(spectrum, valid_mask, bins, band):
    real_part = spectrum[..., :bins]
    imag_part = spectrum[..., bins:]
    power = real_part * real_part + imag_part * imag_part
    band_power = jnp.sum(power.reshape(power.shape[:-1] + (bins // band, band)), axis=-1) / band
    norm_full = jnp.repeat(jnp.sqrt(band_power + 1e-06), band, axis=-1)
    norm_both = jnp.concatenate([norm_full, norm_full], axis=-1)
    return (spectrum / norm_both * valid_mask[..., None].astype(jnp.float32)).astype(jnp.bfloat16)


def cross_block(rows, pair_entry, block, bins):
    first_rows = lax.dynamic_slice_in_dim(rows, pair_entry[0] * block, block, 1).astype(jnp.float32)
    second_rows = lax.dynamic_slice_in_dim(rows, pair_entry[1] * block, block, 1).astype(
        jnp.float32
    )
    first_real = first_rows[..., :bins]
    first_imag = first_rows[..., bins:]
    second_real = second_rows[..., :bins]
    second_imag = second_rows[..., bins:]
    cross_real = jnp.sum(first_real * second_real + first_imag * second_imag, axis=0)
    cross_imag = jnp.sum(first_real * second_imag - first_imag * second_real, axis=0)
    return jnp.concatenate([cross_real, cross_imag], axis=-1)


def local(strain, valid_mask, pair_list, owner_group):
    window_count = strain.shape[0]
    groups = lax.axis_size("grp")
    forward = forward_table(NFFT, NB)
    spectrum = jnp.dot(strain.reshape(-1, NFFT), forward, preferred_element_type=jnp.float32)
    spectrum = spectrum.reshape(strain.shape[0], strain.shape[1], 2 * NB)
    white = whiten_rows(spectrum, valid_mask, NB, SUB)
    gathered = lax.all_gather(white, "ch", axis=1, tiled=True)
    pair_codes = pair_list[0]
    partial_value = lax.map(
        lambda pair_entry: cross_block(gathered, pair_entry, BLK, NB), pair_codes
    )
    owners = owner_group[0]
    list_len = owners.shape[0]
    positions = jnp.arange(list_len, dtype=jnp.int32)
    earlier = positions[None, :] < positions[:, None]
    slot_rank = jnp.sum(((owners[:, None] == owners[None, :]) & earlier).astype(jnp.int32), axis=1)
    slot_ids = jnp.arange(CAP, dtype=jnp.int32)
    flat_partial = partial_value.reshape(list_len, -1)
    summed = lax.psum(flat_partial, "grp")
    my_group = lax.axis_index("grp")
    picking = ((owners[None, :] == my_group) & (slot_rank[None, :] == slot_ids[:, None])).astype(
        jnp.float32
    )
    total = jnp.dot(
        picking, summed, precision=lax.Precision.HIGHEST, preferred_element_type=jnp.float32
    )
    inverse = inverse_table(NFFT, NB)
    stacked = jnp.dot(
        total.reshape(-1, 2 * NB),
        inverse,
        precision=lax.Precision.HIGHEST,
        preferred_element_type=jnp.float32,
    )
    scale = 1.0 / math.sqrt(NB * window_count * groups)
    return (stacked * scale).reshape(1, 1, CAP, BLK, NFFT)


def solution(mesh):
    placed = (P("grp", "ch", None), P("grp", "ch"), P("ch", None, None), P("ch", None))
    return jax.shard_map(
        local,
        mesh=mesh,
        in_specs=placed,
        out_specs=P("grp", "ch", None, None, None),
        check_vma=False,
    )
```

profile of v0, /device:TPU:0, one launch (start us, length us, event | category | flops | bytes accessed | tf_op | source)
XLA Modules:
  0.0 475.3 jit_solution(4424673960620839761)
XLA Ops:
  6.5 0.1 multiply_subtract_fusion
  6.6 0.8 convert_element_type.43
  7.4 69.9 %multiply_convert_fusion.1 = (bf16[4096,1024]{1,0:T(8,128)(2,1)}, bf16[4096,1024]{1,0:T(8,128)(2,1)}) fusion(s32[1024]{0:T(1024)S(1)} %iota_add_fusion.1, f32[4096]{0:T(1024)S(1)} %get-tuple-element.54, f32[4096]{0:T(1024)S(1)} %get-tuple-element.55), kind=kLoop, calls=%fused_computation.31 | loop fusion | flops 75497472 | bytes 16814080 | tf_op jit(solution)/shard_map/convert
  77.4 9.8 %fusion.11 = f32[2048,256]{0,1:T(8,128)} fusion(bf16[256,4096]{1,0:T(8,128)(2,1)S(1)} %bitcast.29, bf16[4096,1024]{1,0:T(8,128)(2,1)} %get-tuple-element.53, bf16[4096,1024]{1,0:T(8,128)(2,1)} %get-tuple-element.52), kind=kOutput, calls=%fused_computation.25 | convolution fusion | flops 4328521728 | bytes 20971520 | tf_op jit(solution)/shard_map/dot_general | solution.py:63
  87.2 1.9 copy.11
  89.1 0.2 bitcast_reduce_fusion
  89.5 1.2 fusion.23
  90.7 0.2 all-reduce.2.cloned.1.call-start
  91.0 127.6 %all-gather.2.cloned.1.call-done = bf16[2,1024,2048]{1,2,0:T(8,128)(2,1)} async-done(((bf16[2,128,2048]{1,2,0:T(8,128)(2,1)}), bf16[2,1024,2048]{1,2,0:T(8,128)(2,1)}) %all-gather.2.cloned.1.call-update) | async-done | bytes 8388624 | tf_op jit(solution)/shard_map/all_gather | solution.py:66
  218.5 11.7 %copy.12 = bf16[2,1024,2048]{2,1,0:T(8,128)(2,1)} copy(bf16[2,1024,2048]{1,2,0:T(8,128)(2,1)} %all-gather.2.cloned.1.call-done) | data formatting | bytes 16777216 | tf_op jit(solution)/shard_map/while | solution.py:68
  230.2 32.5 %while.10 = (s32[]{:T(128)}, f32[6,128,2048]{2,1,0:T(8,128)}, s32[6,2]{0,1:T(2,128)S(1)}, bf16[2,1024,2048]{2,1,0:T(8,128)(2,1)}, s32[]{:T(128)}, /*index=5*/s32[1,1]{0,1:T(1,128)}, s32[]{:T(128)}, s32[]{:T(128)}) while((s32[]{:T(128)}, f32[6,128,2048]{2,1,0:T(8,128)}, s32[6,2]{0,1:T(2,128)S(1)}, bf16[2,1024,2048]{2,1,0:T(8,128)(2,1)}, ...), condition=%wide.region_5.6_spmd, body=%wide.region_2.0_spmd.sunk | while | flops 3145738 | bytes 13631721 | solution.py:68
  230.2 0.1 constant_dynamic-slice_fusion.2
  230.3 0.5 fusion.41
  232.1 1.9 dynamic-slice_convert_fusion.3
  234.0 0.6 add_reduce_fusion.2
  234.6 1.1 fusion.42
  235.6 0.1 constant_dynamic-slice_fusion.2
  235.7 0.5 fusion.41
  237.5 1.9 dynamic-slice_convert_fusion.3
  239.4 0.6 add_reduce_fusion.2
  240.0 1.1 fusion.42
  241.1 0.1 constant_dynamic-slice_fusion.2
  241.1 0.5 fusion.41
  242.9 1.9 dynamic-slice_convert_fusion.3
  244.8 0.6 add_reduce_fusion.2
  245.4 1.1 fusion.42
  246.5 0.1 constant_dynamic-slice_fusion.2
  246.6 0.5 fusion.41
  248.4 1.9 dynamic-slice_convert_fusion.3
  250.3 0.6 add_reduce_fusion.2
  250.8 1.1 fusion.42
  251.9 0.1 constant_dynamic-slice_fusion.2
  252.0 0.5 fusion.41
  253.8 1.9 dynamic-slice_convert_fusion.3
  255.7 0.6 add_reduce_fusion.2
  256.2 1.1 fusion.42
  257.3 0.1 constant_dynamic-slice_fusion.2
  257.3 0.5 fusion.41
  259.2 1.9 dynamic-slice_convert_fusion.3
  261.0 0.6 add_reduce_fusion.2
  261.6 1.1 fusion.42
  262.7 9.8 %copy.13 = f32[1,6,128,2048]{3,1,2,0:T(8,128)} copy(f32[1,6,128,2048]{3,2,1,0:T(8,128)} %bitcast.31) | data formatting | bytes 12582912
  272.5 0.2 convert_reduce_fusion
  272.7 68.4 %fusion.18 = (f32[1024,4096]{1,0:T(8,128)}, f32[1024,4096]{1,0:T(8,128)}) fusion(s32[4096]{0:T(1024)S(1)} %iota_add_fusion, s32[1024]{0:T(1024)S(1)} %iota_add_fusion.1), kind=kLoop, calls=%fused_computation.35 | loop fusion | flops 62914560 | bytes 33574912 | tf_op jit(solution)/shard_map/cos | solution.py:32
  341.2 82.5 %all-reduce.2.cloned.1.call-done = f32[6,262144]{1,0:T(8,128)} async-done(((f32[6,262144]{1,0:T(8,128)}), f32[6,262144]{1,0:T(8,128)}) %all-reduce.2.cloned.1.call-update) | async-done | bytes 6291472 | tf_op jit(solution)/shard_map/psum | solution.py:78
  423.7 7.4 %fusion.27 = f32[2,262144]{1,0:T(2,128)S(1)} fusion(f32[6,262144]{1,0:T(8,128)} %all-reduce.2.cloned.1.call-done, pred[6]{0:T(512)(128)(4,1)S(1)} %compare_bitcast_fusion, s32[6]{0:T(128)S(1)} %convert_reduce_fusion), kind=kOutput, calls=%fused_computation.52 | convolution fusion | flops 37748760 | bytes 8388638 | tf_op jit(solution)/shard_map/dot_general | solution.py:83
  431.1 3.1 reshape.62
  434.2 34.3 %fusion.19 = f32[256,4096]{1,0:T(8,128)} fusion(f32[256,2048]{1,0:T(8,128)} %reshape.62, f32[1024,4096]{1,0:T(8,128)} %get-tuple-element.51, f32[1024,4096]{1,0:T(8,128)} %get-tuple-element.50), kind=kOutput, calls=%fused_computation.36 | convolution fusion | flops 25779240960 | bytes 39845888 | tf_op jit(solution)/shard_map/dot_general | solution.py:87
  (17 shorter events, 0.1 us)
Async XLA Ops:
  6.5 70.9 %copy-start = (bf16[2,128,4096]{2,1,0:T(8,128)(2,1)S(1)}, bf16[2,128,4096]{2,1,0:T(8,128)(2,1)}, u32[]{:S(2)}) copy-start(bf16[2,128,4096]{2,1,0:T(8,128)(2,1)} %param.6) | copy-start | bytes 6291460
  6.5 212.0 %all-gather.2.cloned.1.call-start = ((), (), s32[]{:S(2)}) async-start(), calls=%async_computation | async-start | bytes 9437184 | tf_op jit(solution)/shard_map/all_gather | solution.py:66
  90.7 333.0 %all-reduce.2.cloned.1.call-start = ((), (), s32[]{:S(2)}) async-start(), calls=%async_computation.1 | async-start | bytes 16777216 | tf_op jit(solution)/shard_map/psum | solution.py:78
  91.0 139.3 %copy-start.2 = (s32[1,6,2]{1,2,0:T(2,128)S(1)}, s32[1,6,2]{1,2,0:T(2,128)}, u32[]{:S(2)}) copy-start(s32[1,6,2]{1,2,0:T(2,128)} %param.8) | copy-start | bytes 148
  262.7 9.8 %copy-start.3 = (s32[1,6]{1,0:T(1,128)S(1)}, s32[1,6]{1,0:T(1,128)}, u32[]{:S(2)}) copy-start(s32[1,6]{1,0:T(1,128)} %param.9) | copy-start | bytes 76
  434.2 34.3 %copy-start.1 = (bf16[2,128,4096]{2,1,0:T(8,128)(2,1)S(1)}, bf16[2,128,4096]{2,1,0:T(8,128)(2,1)}, u32[]{:S(2)}) copy-start(bf16[2,128,4096]{2,1,0:T(8,128)(2,1)} %param.6) | copy-start | bytes 6291460
Sparse Core Ops, SparseCore 0:
  90.9 127.6 all-gather.1
  272.6 151.0 all-reduce.1
where the time goes:
time: 476 us; the launch traced here: 475 us
  waiting for transfers between devices  210 us (44%)
  other arithmetic  162 us (34%)
  matrix products  51.5 us (11%)
  local copies, waits for them, and re-layouts  30.2 us (6%)
  between operations  13.5 us (3%)
  loops' own time  7.78 us (2%)
    all_gather x1, waiting for transfers between devices, local(): gathered = lax.all_gather(white, 'ch', axis=1, tiled=True)  128 us
    psum x1, waiting for transfers between devices, local(): summed = lax.psum(flat_partial, 'grp')  82.5 us
    another operation x1, other arithmetic  69.9 us
    cos x1, other arithmetic, inverse_table(): return jnp.concatenate([jnp.cos(angles), -jnp.sin(angles)], axis=0)  68.4 us
    dot_general x1, matrix products, local(): jnp.dot(total.reshape(-1, 2 * NB), inverse, precision=lax.Precision.HIGHE...  34.3 us
    while x1, local copies, waits for them, and re-layouts, local(): lax.map(lambda pair_entry: cross_block(gathered, pair_entry, BLK, NB), pa...  11.7 us
    convert_element_type x6, other arithmetic, cross_block(): lax.dynamic_slice_in_dim(rows, pair_entry[0] * block, block, 1)  11.3 us
    dot_general x1, matrix products, local(): jnp.dot(strain.reshape(-1, NFFT), forward, preferred_element_type=jnp.flo...  9.8 us
  transfers between devices with their start and end apart: 2, of which 2 were waited for; matrix products, arithmetic and copies ran while one was open for 14% of the time, Pallas kernels for 0%

commit v1 on v0

--- a/solution.py
+++ b/solution.py
@@ -63,7 +63,23 @@
     spectrum = jnp.dot(strain.reshape(-1, NFFT), forward, preferred_element_type=jnp.float32)
     spectrum = spectrum.reshape(strain.shape[0], strain.shape[1], 2 * NB)
     white = whiten_rows(spectrum, valid_mask, NB, SUB)
-    gathered = lax.all_gather(white, "ch", axis=1, tiled=True)
+    size, index, extent = (lax.axis_size("ch"), lax.axis_index("ch"), white.shape[1])
+    right = [(i, (i + 1) % size) for i in range(size)]
+    left = [(i, (i - 1) % size) for i in range(size)]
+    gathered = jnp.zeros((*white.shape[:1], size * extent, *white.shape[1 + 1 :]), white.dtype)
+    gathered = lax.dynamic_update_slice_in_dim(gathered, white, index * extent, axis=1)
+    from_left = from_right = white
+    half = size // 2
+    for step in range(1, half + 1):
+        from_left = lax.ppermute(from_left, "ch", right)
+        gathered = lax.dynamic_update_slice_in_dim(
+            gathered, from_left, (index - step) % size * extent, axis=1
+        )
+        if step < size - half:
+            from_right = lax.ppermute(from_right, "ch", left)
+            gathered = lax.dynamic_update_slice_in_dim(
+                gathered, from_right, (index + step) % size * extent, axis=1
+            )
     pair_codes = pair_list[0]
     partial_value = lax.map(
         lambda pair_entry: cross_block(gathered, pair_entry, BLK, NB), pair_codes

time: 476 us -> 505 us (1.061)
  starting transfers between devices: 0.22 us -> 19.9 us
  local copies, waits for them, and re-layouts: 30.2 us -> 39.9 us
    ppermute x0 -> x7, waiting for transfers between devices: none -> 128 us  [the longest x4 128 us: local(): from_left = lax.ppermute(from_left, 'ch', right)]
    all_gather x1 -> x0, waiting for transfers between devices: 128 us -> none  [local(): gathered = lax.all_gather(white, 'ch', axis=1, tiled=True)]
    ppermute x0 -> x7, starting transfers between devices: none -> 19.9 us  [the longest x4 10.6 us: local(): from_left = lax.ppermute(from_left, 'ch', right)]
    while x1 -> x0, local copies, waits for them, and re-layouts: 11.7 us -> none  [local(): lax.map(lambda pair_entry: cross_block(gathered, pair_entry, BLK, NB), pa...]
    dynamic_update_slice x0 -> x8, local copies, waits for them, and re-layouts: none -> 8.66 us  [the longest x4 4.36 us: local(): lax.dynamic_update_slice_in_dim(gathered, from_left, (index - step) % siz...]
    ppermute x0 -> x7, local copies, waits for them, and re-layouts: none -> 7.51 us  [the longest x4 4.02 us: local(): from_left = lax.ppermute(from_left, 'ch', right)]
  transfers between devices with their start and end apart: 2 -> 8, of which waited for: 2 -> 5; matrix products, arithmetic and copies ran while one was open for 14% -> 17% of each run, Pallas kernels for 0% -> 0%
where the time goes in v1:
time: 505 us
  waiting for transfers between devices  211 us (42%)
  other arithmetic  161 us (32%)
  matrix products  51.5 us (10%)
  local copies, waits for them, and re-layouts  39.9 us (8%)
  starting transfers between devices  19.9 us (4%)
  between operations  13.6 us (3%)
  loops' own time  8.19 us (2%)
    ppermute x4, waiting for transfers between devices, local(): from_left = lax.ppermute(from_left, 'ch', right)  128 us
    psum x1, waiting for transfers between devices, local(): summed = lax.psum(flat_partial, 'grp')  83 us
    another operation x1, other arithmetic  69.9 us
    cos x1, other arithmetic, inverse_table(): return jnp.concatenate([jnp.cos(angles), -jnp.sin(angles)], axis=0)  68.4 us
    dot_general x1, matrix products, local(): jnp.dot(total.reshape(-1, 2 * NB), inverse, precision=lax.Precision.HIGHE...  34.3 us
    convert_element_type x6, other arithmetic, cross_block(): lax.dynamic_slice_in_dim(rows, pair_entry[0] * block, block, 1)  11.3 us
    ppermute x4, starting transfers between devices, local(): from_left = lax.ppermute(from_left, 'ch', right)  10.6 us
  transfers between devices with their start and end apart: 8, of which 5 were waited for; matrix products, arithmetic and copies ran while one was open for 17% of the time, Pallas kernels for 0%

profile of v1, /device:TPU:0, one launch (start us, length us, event | category | flops | bytes accessed | tf_op | source)
XLA Modules:
  0.0 504.8 jit_solution(5393247847474710143)
XLA Ops:
  6.6 0.8 convert_element_type.43
  7.4 69.9 %multiply_convert_fusion.1 = (bf16[4096,1024]{1,0:T(8,128)(2,1)}, bf16[4096,1024]{1,0:T(8,128)(2,1)}) fusion(s32[1024]{0:T(1024)S(1)} %iota_add_fusion.1, f32[4096]{0:T(1024)S(1)} %get-tuple-element.46, f32[4096]{0:T(1024)S(1)} %get-tuple-element.47), kind=kLoop, calls=%fused_computation.31 | loop fusion | flops 75497472 | bytes 16814080 | tf_op jit(solution)/shard_map/convert
  77.4 9.8 %fusion.11 = f32[2048,256]{0,1:T(8,128)} fusion(bf16[256,4096]{1,0:T(8,128)(2,1)S(1)} %bitcast.29, bf16[4096,1024]{1,0:T(8,128)(2,1)} %get-tuple-element.45, bf16[4096,1024]{1,0:T(8,128)(2,1)} %get-tuple-element.44), kind=kOutput, calls=%fused_computation.25 | convolution fusion | flops 4328521728 | bytes 20971520 | tf_op jit(solution)/shard_map/dot_general | solution.py:63
  87.2 1.9 copy.18
  89.7 3.0 collective-permute-start
  92.8 3.1 collective-permute-start.1
  95.9 41.8 %collective-permute-done = bf16[2,128,2048]{1,2,0:T(8,128)(2,1)S(1)} collective-permute-done((bf16[2,128,2048]{1,2,0:T(8,128)(2,1)S(1)}, bf16[2,128,2048]{1,2,0:T(8,128)(2,1)S(1)}, u32[]{:S(2)}, u32[]{:S(2)}) %collective-permute-start) | collective-permute-done | bytes 1048608 | tf_op jit(solution)/shard_map/ppermute | solution.py:74
  137.6 2.5 collective-permute-start.2
  140.1 3.1 collective-permute-start.3
  143.2 40.9 %collective-permute-done.2 = bf16[2,128,2048]{1,2,0:T(8,128)(2,1)} collective-permute-done((bf16[2,128,2048]{1,2,0:T(8,128)(2,1)S(1)}, bf16[2,128,2048]{1,2,0:T(8,128)(2,1)}, u32[]{:S(2)}, u32[]{:S(2)}) %collective-permute-start.2) | collective-permute-done | bytes 1048608 | tf_op jit(solution)/shard_map/ppermute | solution.py:74
  184.2 2.6 collective-permute-start.4
  187.3 3.1 collective-permute-start.5
  190.4 4.3 broadcast_in_dim.11
  194.7 1.1 constant_dynamic-update-slice_fusion.7
  196.9 1.1 constant_dynamic-update-slice_fusion.6
  198.0 32.4 %collective-permute-done.4 = bf16[2,128,2048]{1,2,0:T(8,128)(2,1)} collective-permute-done((bf16[2,128,2048]{1,2,0:T(8,128)(2,1)}, bf16[2,128,2048]{1,2,0:T(8,128)(2,1)}, u32[]{:S(2)}, u32[]{:S(2)}) %collective-permute-start.4) | collective-permute-done | bytes 1048608 | tf_op jit(solution)/shard_map/ppermute | solution.py:74
  230.4 2.5 collective-permute-start.6
  232.9 1.1 constant_dynamic-update-slice_fusion.5
  234.0 1.5 copy.23
  235.4 1.5 copy.22
  236.9 1.1 constant_dynamic-update-slice_fusion.4
  238.0 1.1 constant_dynamic-update-slice_fusion.3
  239.1 1.5 copy.24
  240.6 1.5 copy.25
  242.1 1.1 constant_dynamic-update-slice_fusion.2
  243.2 1.1 constant_dynamic-update-slice_fusion.1
  244.2 12.5 %collective-permute-done.6 = bf16[2,128,2048]{1,2,0:T(8,128)(2,1)S(1)} collective-permute-done((bf16[2,128,2048]{1,2,0:T(8,128)(2,1)}, bf16[2,128,2048]{1,2,0:T(8,128)(2,1)S(1)}, u32[]{:S(2)}, u32[]{:S(2)}) %collective-permute-start.6) | collective-permute-done | bytes 1048608 | tf_op jit(solution)/shard_map/ppermute | solution.py:74
  257.3 1.1 constant_dynamic-update-slice_fusion
  258.3 33.3 %while.10 = (s32[]{:T(128)}, f32[6,128,2048]{2,1,0:T(8,128)}, s32[6,2]{0,1:T(2,128)S(1)}, bf16[2,1024,2048]{2,1,0:T(8,128)(2,1)}, s32[]{:T(128)}, /*index=5*/s32[1,1]{0,1:T(1,128)}, s32[]{:T(128)}, s32[]{:T(128)}) while((s32[]{:T(128)}, f32[6,128,2048]{2,1,0:T(8,128)}, s32[6,2]{0,1:T(2,128)S(1)}, bf16[2,1024,2048]{2,1,0:T(8,128)(2,1)}, ...), condition=%wide.region_5.6_spmd, body=%wide.region_2.5_spmd.sunk | while | flops 3145738 | bytes 13631721 | solution.py:84
  258.4 0.6 fusion.41
  260.4 1.9 dynamic-slice_convert_fusion.3
  262.8 1.1 fusion.42
  266.0 1.9 dynamic-slice_convert_fusion.3
  268.4 1.0 fusion.42
  271.5 1.9 dynamic-slice_convert_fusion.3
  273.9 1.1 fusion.42
  277.0 1.9 dynamic-slice_convert_fusion.3
  279.5 1.1 fusion.42
  282.6 1.9 dynamic-slice_convert_fusion.3
  285.0 1.1 fusion.42
  288.2 1.9 dynamic-slice_convert_fusion.3
  290.6 1.1 fusion.42
  291.7 9.8 %copy.27 = f32[1,6,128,2048]{3,1,2,0:T(8,128)} copy(f32[1,6,128,2048]{3,2,1,0:T(8,128)} %bitcast.31) | data formatting | bytes 12582912
  301.7 68.4 %fusion.18 = (f32[1024,4096]{1,0:T(8,128)}, f32[1024,4096]{1,0:T(8,128)}) fusion(s32[4096]{0:T(1024)S(1)} %iota_add_fusion, s32[1024]{0:T(1024)S(1)} %iota_add_fusion.1), kind=kLoop, calls=%fused_computation.35 | loop fusion | flops 62914560 | bytes 33574912 | tf_op jit(solution)/shard_map/cos | solution.py:32
  370.1 83.0 %all-reduce.2.cloned.1.call-done = f32[6,262144]{1,0:T(8,128)} async-done(((f32[6,262144]{1,0:T(8,128)}), f32[6,262144]{1,0:T(8,128)}) %all-reduce.2.cloned.1.call-update) | async-done | bytes 6291472 | tf_op jit(solution)/shard_map/psum | solution.py:94
  453.1 7.4 %fusion.27 = f32[2,262144]{1,0:T(2,128)S(1)} fusion(f32[6,262144]{1,0:T(8,128)} %all-reduce.2.cloned.1.call-done, pred[6]{0:T(512)(128)(4,1)S(1)} %compare_bitcast_fusion, s32[6]{0:T(128)S(1)} %convert_reduce_fusion), kind=kOutput, calls=%fused_computation.60 | convolution fusion | flops 37748760 | bytes 8388638 | tf_op jit(solution)/shard_map/dot_general | solution.py:99
  460.6 3.1 reshape.62
  463.7 34.3 %fusion.19 = f32[256,4096]{1,0:T(8,128)} fusion(f32[256,2048]{1,0:T(8,128)} %reshape.62, f32[1024,4096]{1,0:T(8,128)} %get-tuple-element.43, f32[1024,4096]{1,0:T(8,128)} %get-tuple-element.42), kind=kOutput, calls=%fused_computation.36 | convolution fusion | flops 25779240960 | bytes 39845888 | tf_op jit(solution)/shard_map/dot_general | solution.py:103
  (48 shorter events, 9.8 us)
Async XLA Ops:
  6.5 70.8 %copy-start = (bf16[2,128,4096]{2,1,0:T(8,128)(2,1)S(1)}, bf16[2,128,4096]{2,1,0:T(8,128)(2,1)}, u32[]{:S(2)}) copy-start(bf16[2,128,4096]{2,1,0:T(8,128)(2,1)} %param.6) | copy-start | bytes 6291460
  6.5 446.6 %all-reduce.2.cloned.1.call-start = ((), (), s32[]{:S(2)}) async-start(), calls=%async_computation | async-start | bytes 16777216 | tf_op jit(solution)/shard_map/psum | solution.py:94
  89.7 47.9 %collective-permute-start = (bf16[2,128,2048]{1,2,0:T(8,128)(2,1)S(1)}, bf16[2,128,2048]{1,2,0:T(8,128)(2,1)S(1)}, u32[]{:S(2)}, u32[]{:S(2)}) collective-permute-start(bf16[2,128,2048]{1,2,0:T(8,128)(2,1)S(1)} %fusion.23), channel_id=1, source_target_pairs={{0,1},{1,2},{2,3},{3,4},{4,5},{5,6},{6,7},{7,0},{8,9},{9,10},{10,1... | collective-permute-start | bytes 3145736 | tf_op jit(solution)/shard_map/ppermute | solution.py:74
  92.8 47.4 %collective-permute-start.1 = (bf16[2,128,2048]{1,2,0:T(8,128)(2,1)S(1)}, bf16[2,128,2048]{1,2,0:T(8,128)(2,1)S(1)}, u32[]{:S(2)}, u32[]{:S(2)}) collective-permute-start(bf16[2,128,2048]{1,2,0:T(8,128)(2,1)S(1)} %fusion.23), channel_id=1, source_target_pairs={{0,7},{1,0},{2,1},{3,2},{4,3},{5,4},{6,5},{7,6},{8,15},{9,8},{10,9... | collective-permute-start | bytes 3145736 | tf_op jit(solution)/shard_map/ppermute | solution.py:79
  137.6 49.1 %copy-start.2 = (bf16[2,128,2048]{1,2,0:T(8,128)(2,1)}, bf16[2,128,2048]{1,2,0:T(8,128)(2,1)S(1)}, u32[]{:S(2)}) copy-start(bf16[2,128,2048]{1,2,0:T(8,128)(2,1)S(1)} %collective-permute-done) | copy-start | bytes 3145732
  137.6 46.5 %collective-permute-start.2 = (bf16[2,128,2048]{1,2,0:T(8,128)(2,1)S(1)}, bf16[2,128,2048]{1,2,0:T(8,128)(2,1)}, u32[]{:S(2)}, u32[]{:S(2)}) collective-permute-start(bf16[2,128,2048]{1,2,0:T(8,128)(2,1)S(1)} %collective-permute-done), channel_id=1, source_target_pairs={{0,1},{1,2},{2,3},{3,4},{4,5},{5,6},{6,7},{7,0},{8,9},{9,10},{10,1... | collective-permute-start | bytes 3145736 | tf_op jit(solution)/shard_map/ppermute | solution.py:74
  140.1 47.2 %collective-permute-start.3 = (bf16[2,128,2048]{1,2,0:T(8,128)(2,1)S(1)}, bf16[2,128,2048]{1,2,0:T(8,128)(2,1)}, u32[]{:S(2)}, u32[]{:S(2)}) collective-permute-start(bf16[2,128,2048]{1,2,0:T(8,128)(2,1)S(1)} %collective-permute-done.1), channel_id=1, source_target_pairs={{0,7},{1,0},{2,1},{3,2},{4,3},{5,4},{6,5},{7,6},{8,15},{9,8},{10,9... | collective-permute-start | bytes 3145736 | tf_op jit(solution)/shard_map/ppermute | solution.py:79
  184.2 46.2 %collective-permute-start.4 = (bf16[2,128,2048]{1,2,0:T(8,128)(2,1)}, bf16[2,128,2048]{1,2,0:T(8,128)(2,1)}, u32[]{:S(2)}, u32[]{:S(2)}) collective-permute-start(bf16[2,128,2048]{1,2,0:T(8,128)(2,1)} %collective-permute-done.2), channel_id=1, source_target_pairs={{0,1},{1,2},{2,3},{3,4},{4,5},{5,6},{6,7},{7,0},{8,9},{9,10},{10,1... | collective-permute-start | bytes 3145736 | tf_op jit(solution)/shard_map/ppermute | solution.py:74
  187.3 9.0 %copy-start.3 = (bf16[2,128,2048]{1,2,0:T(8,128)(2,1)S(1)}, bf16[2,128,2048]{1,2,0:T(8,128)(2,1)}, u32[]{:S(2)}) copy-start(bf16[2,128,2048]{1,2,0:T(8,128)(2,1)} %copy-done.2) | copy-start | bytes 3145732
  187.3 53.3 %collective-permute-start.5 = (bf16[2,128,2048]{1,2,0:T(8,128)(2,1)}, bf16[2,128,2048]{1,2,0:T(8,128)(2,1)}, u32[]{:S(2)}, u32[]{:S(2)}) collective-permute-start(bf16[2,128,2048]{1,2,0:T(8,128)(2,1)} %collective-permute-done.3), channel_id=1, source_target_pairs={{0,7},{1,0},{2,1},{3,2},{4,3},{5,4},{6,5},{7,6},{8,15},{9,8},{10,9... | collective-permute-start | bytes 3145736 | tf_op jit(solution)/shard_map/ppermute | solution.py:79
  230.4 26.3 %collective-permute-start.6 = (bf16[2,128,2048]{1,2,0:T(8,128)(2,1)}, bf16[2,128,2048]{1,2,0:T(8,128)(2,1)S(1)}, u32[]{:S(2)}, u32[]{:S(2)}) collective-permute-start(bf16[2,128,2048]{1,2,0:T(8,128)(2,1)} %collective-permute-done.4), channel_id=1, source_target_pairs={{0,1},{1,2},{2,3},{3,4},{4,5},{5,6},{6,7},{7,0},{8,9},{9,10},{10,1... | collective-permute-start | bytes 3145736 | tf_op jit(solution)/shard_map/ppermute | solution.py:74
  236.9 21.4 %copy-start.4 = (s32[1,6,2]{1,2,0:T(2,128)S(1)}, s32[1,6,2]{1,2,0:T(2,128)}, u32[]{:S(2)}) copy-start(s32[1,6,2]{1,2,0:T(2,128)} %param.8) | copy-start | bytes 148
  291.7 9.8 %copy-start.5 = (s32[1,6]{1,0:T(1,128)S(1)}, s32[1,6]{1,0:T(1,128)}, u32[]{:S(2)}) copy-start(s32[1,6]{1,0:T(1,128)} %param.9) | copy-start | bytes 76
  463.7 34.3 %copy-start.1 = (bf16[2,128,4096]{2,1,0:T(8,128)(2,1)S(1)}, bf16[2,128,4096]{2,1,0:T(8,128)(2,1)}, u32[]{:S(2)}) copy-start(bf16[2,128,4096]{2,1,0:T(8,128)(2,1)} %param.6) | copy-start | bytes 6291460
Sparse Core Ops, SparseCore 0:
  301.6 151.4 all-reduce.1
